TPU v7x, 32 devices: a whole 2x2x4 slice. The times are simulated.
32 devices in a mesh: row: 1, ang: 32 (over z, y, x, core).
Axes of the slice: x: 2, y: 2, z: 4, core: 2. Of those that a mesh axis runs over, the one named last changes fastest.
Arguments:
- linv_t: bfloat16 [2, 2048, 2048], P(None, 'ang', 'row'), may hold values from -1.5 to 1.5, as said below
- rhs_top: float32 [2, 2048, 16384], P(None, 'row', 'ang'), may hold values from -6 to 6
- factor_t: bfloat16 [2, 2048, 1024], P(None, 'ang', 'row'), may hold values from -0.125 to 0.125
- rhs_rest: float32 [2, 1024, 16384], P(None, 'row', 'ang'), may hold values from -6 to 6
Outputs:
- solved: float32 [2, 2048, 16384], P(None, 'row', 'ang')
- updated: float32 [2, 1024, 16384], P(None, 'row', 'ang')
Inputs may be any that keep to these rules, and one draw needn't show every extreme that they name: `linv_t`: lower triangular inverse: entry [c, j, i] is zero where j > i; the diagonal is real and between 0.5 and 1.5.
All inputs are finite; a program needn't handle non-finite values.
Results may differ from a plain program's by a relative error of at most 0.0026.
Values may be sent and summed in bfloat16 or wider, within the bound.
A program may use at most 128 MiB of HBM per device.

v0:
```python
import functools

import jax
import jax.numpy as jnp
from jax import lax
from jax.experimental import pallas as pl
from jax.experimental.pallas import tpu as pltpu
from jax.sharding import PartitionSpec as P

BLOCK = 256
KINDS = ((0, 0, "zyx"), (0, 1, "zxy"), (1, 0, "yzx"), (1, 1, "xzy"))
DIMS0 = (((0,), (0,)), ((), ()))


def tdot(first, second):
    return lax.dot_general(first, second, DIMS0, preferred_element_type=jnp.float32)


def split_two(value):
    high = value.astype(jnp.bfloat16)
    low = (value - high.astype(jnp.float32)).astype(jnp.bfloat16)
    return high, low


def general_body(linv_t, rhs_top, factor_t, rhs_rest):
    top_all = lax.all_gather(rhs_top, "row", axis=1, tiled=True)
    high, low = split_two(top_all)
    inverse = lax.all_gather(linv_t, "ang", axis=1, tiled=True)

    def single(first, second):
        return tdot(inverse[first], high[second]) + tdot(inverse[first], low[second])

    solved = jnp.stack([single(0, 0) - single(1, 1), single(0, 1) + single(1, 0)])
    half = lax.all_gather(solved.astype(jnp.bfloat16), "row", axis=1, tiled=True)
    factor = lax.all_gather(factor_t, "ang", axis=1, tiled=True)
    update = jnp.stack(
        [
            tdot(factor[0], half[0]) - tdot(factor[1], half[1]),
            tdot(factor[0], half[1]) + tdot(factor[1], half[0]),
        ]
    )
    return (solved, rhs_rest - update)


def gather_kernel(devices, lin_ref, fac_ref, glin, gfac, recv, send, local):
    levels = devices // 8
    rows = lin_ref.shape[1]
    panel = lin_ref.shape[2]
    classes = panel // BLOCK
    per_class = BLOCK // rows

    me = lax.axis_index("ang")
    core = lax.rem(me, 2)
    x = lax.rem(me // 2, 2)
    y = lax.rem(me // 4, 2)
    z = me // 8
    has_up, has_down = z < levels - 1, z > 0
    targets = (
        me + 2 - 4 * x,
        me + 4 - 8 * y,
        jnp.where(has_up, me + 8, me),
        jnp.where(has_down, me - 8, me),
        me + 1 - 2 * core,
    )

    barrier = pltpu.get_barrier_semaphore()

    def greet(target):
        pl.semaphore_signal(
            barrier, inc=1, device_id={"ang": target}, device_id_type=pl.DeviceIdType.MESH
        )

    for index in (0, 1, 4):
        greet(targets[index])
    pl.when(has_up)(lambda: greet(targets[2]))
    pl.when(has_down)(lambda: greet(targets[3]))
    pl.semaphore_wait(barrier, 3 + has_up.astype(jnp.int32) + has_down.astype(jnp.int32))

    def place(kind, origin, cls):
        which, part, _ = KINDS[kind]
        at_rows = pl.ds(pl.multiple_of(origin * rows, rows), rows)
        if which == 0:
            return glin.at[part, at_rows, pl.ds(cls * BLOCK, panel - cls * BLOCK)]
        return gfac.at[part, at_rows, :]

    def source(kind, cls):
        which, part, _ = KINDS[kind]
        if which == 0:
            return lin_ref.at[part, :, pl.ds(cls * BLOCK, panel - cls * BLOCK)]
        return fac_ref.at[part]

    def by_class(kind, origin, action):
        if KINDS[kind][0] == 0:
            for cls in range(classes):
                pl.when(origin // per_class == cls)(functools.partial(action, cls))
        else:
            action(0)

    def remote(kind, origin, cls, direction, own):
        return pltpu.make_async_remote_copy(
            src_ref=source(kind, cls) if own else place(kind, origin, cls),
            dst_ref=place(kind, origin, cls),
            send_sem=send.at[direction, kind, origin // 2],
            recv_sem=recv.at[kind, origin],
            device_id={"ang": targets[direction]},
            device_id_type=pl.DeviceIdType.MESH,
        )

    def onward(kind, zo, yo, xo):
        same = {"x": x == xo, "y": y == yo, "z": z == zo}
        order = KINDS[kind][2]
        free = {}
        for position, axis in enumerate(order):
            ok = True
            for later in order[position + 1 :]:
                ok = same[later] if ok is True else jnp.logical_and(ok, same[later])
            free[axis] = ok

        def both(first, second):
            return second if first is True else jnp.logical_and(first, second)

        return (
            both(free["x"], same["x"]),
            both(free["y"], same["y"]),
            both(free["z"], jnp.logical_and(z >= zo, has_up)),
            both(free["z"], jnp.logical_and(z <= zo, has_down)),
            True,
        )

    def forward(kind, origin, goes, cls, own, act):
        for direction in range(5):
            copy = remote(kind, origin, cls, direction, own)
            run = copy.start if act == "start" else copy.wait_send
            if goes[direction] is True:
                run()
            else:
                pl.when(goes[direction])(run)

    for kind in range(4):
        goes = onward(kind, z, y, x)
        by_class(kind, me, lambda cls, kind=kind, goes=goes: forward(kind, me, goes, cls, True, "start"))
    copies = (
        pltpu.make_async_copy(lin_ref, glin.at[:, pl.ds(pl.multiple_of(me * rows, rows), rows), :], local.at[0]),
        pltpu.make_async_copy(fac_ref, gfac.at[:, pl.ds(pl.multiple_of(me * rows, rows), rows), :], local.at[1]),
    )
    for copy in copies:
        copy.start()

    chips = devices // 2
    per_level = levels * 4

    def visit(step, carry):
        hops = step // per_level
        chip = lax.rem(step, per_level)
        zo, yo, xo = chip // 4, lax.rem(chip // 2, 2), lax.rem(chip, 2)
        distance = jnp.abs(z - zo) + jnp.abs(y - yo) + jnp.abs(x - xo)
        origin = chip * 2 + core

        @pl.when(distance == hops)
        def _():
            for kind in range(4):
                goes = onward(kind, zo, yo, xo)

                def arrive(cls, kind=kind, goes=goes):
                    remote(kind, origin, cls, 4, False).wait_recv()
                    forward(kind, origin, goes, cls, False, "start")

                by_class(kind, origin, arrive)

        return carry

    lax.fori_loop(per_level, per_level * (levels + 2), visit, 0)

    def finish(chip, carry):
        zo, yo, xo = chip // 4, lax.rem(chip // 2, 2), lax.rem(chip, 2)
        origin = chip * 2 + core
        other = chip * 2 + 1 - core
        for kind in range(4):
            goes = onward(kind, zo, yo, xo)
            by_class(
                kind,
                origin,
                lambda cls, kind=kind, goes=goes: forward(kind, origin, goes, cls, False, "wait"),
            )
            by_class(
                kind,
                other,
                lambda cls, kind=kind: remote(kind, other, cls, 4, False).wait_recv(),
            )
        return carry

    lax.fori_loop(0, chips, finish, 0)
    for copy in copies:
        copy.wait()


def gather(devices, linv_t, factor_t):
    parts, rows, panel = linv_t.shape
    trail = factor_t.shape[2]
    return pl.pallas_call(
        functools.partial(gather_kernel, devices),
        out_shape=(
            jax.ShapeDtypeStruct((parts, rows * devices, panel), linv_t.dtype),
            jax.ShapeDtypeStruct((parts, rows * devices, trail), factor_t.dtype),
        ),
        in_specs=[pl.BlockSpec(memory_space=pl.ANY)] * 2,
        out_specs=[pl.BlockSpec(memory_space=pl.ANY)] * 2,
        scratch_shapes=[
            pltpu.SemaphoreType.DMA((4, devices)),
            pltpu.SemaphoreType.DMA((5, 4, devices // 2)),
            pltpu.SemaphoreType.DMA((2,)),
        ],
        compiler_params=pltpu.CompilerParams(collective_id=0, has_side_effects=True),
    )(linv_t, factor_t)


def solve_kernel(blocks, lin_ref, top_ref, fac_ref, rest_ref, solved_ref, updated_ref, high, low, half, acc):
    step = pl.program_id(0)
    width = top_ref.shape[2]

    @pl.when(step == 0)
    def _():
        @pl.loop(0, blocks)
        def _(index):
            at_rows = pl.ds(pl.multiple_of(index * BLOCK, BLOCK), BLOCK)
            for part in range(2):
                first, second = split_two(top_ref[part, at_rows, :])
                high[at_rows, part * width : (part + 1) * width] = first
                low[at_rows, part * width : (part + 1) * width] = second

    def add(real, imag):
        acc[:, :width] += real[:, :width] - imag[:, width:]
        acc[:, width:] += real[:, width:] + imag[:, :width]

    acc[...] = jnp.zeros_like(acc)

    @pl.when(step < blocks)
    def _():
        @pl.loop(0, step + 1)
        def _(index):
            at_rows = pl.ds(pl.multiple_of(index * BLOCK, BLOCK), BLOCK)
            first, second = high[at_rows, :], low[at_rows, :]
            lreal, limag = lin_ref[0, at_rows, :], lin_ref[1, at_rows, :]
            add(
                tdot(lreal, first) + tdot(lreal, second),
                tdot(limag, first) + tdot(limag, second),
            )

        solved_ref[0] = acc[:, :width]
        solved_ref[1] = acc[:, width:]
        half[pl.ds(pl.multiple_of(step * BLOCK, BLOCK), BLOCK), :] = acc[...].astype(jnp.bfloat16)

    @pl.when(step >= blocks)
    def _():
        @pl.loop(0, blocks)
        def _(index):
            at_rows = pl.ds(pl.multiple_of(index * BLOCK, BLOCK), BLOCK)
            right = half[at_rows, :]
            add(tdot(fac_ref[0, at_rows, :], right), tdot(fac_ref[1, at_rows, :], right))

        updated_ref[0] = rest_ref[0] - acc[:, :width]
        updated_ref[1] = rest_ref[1] - acc[:, width:]


def solve(lin, top, fac, rest):
    parts, panel, width = top.shape
    trail = rest.shape[1]
    blocks, tail = panel // BLOCK, trail // BLOCK
    once = pl.Buffered(1)
    return pl.pallas_call(
        functools.partial(solve_kernel, blocks),
        grid=(blocks + tail,),
        out_shape=(
            jax.ShapeDtypeStruct(top.shape, jnp.float32),
            jax.ShapeDtypeStruct(rest.shape, jnp.float32),
        ),
        in_specs=[
            pl.BlockSpec((parts, panel, BLOCK), lambda i: (0, 0, jnp.minimum(i, blocks - 1))),
            pl.BlockSpec((parts, panel, width), lambda i: (0, 0, 0), pipeline_mode=once),
            pl.BlockSpec((parts, panel, BLOCK), lambda i: (0, 0, jnp.maximum(i - blocks, 0))),
            pl.BlockSpec((parts, BLOCK, width), lambda i: (0, jnp.maximum(i - blocks, 0), 0)),
        ],
        out_specs=[
            pl.BlockSpec((parts, BLOCK, width), lambda i: (0, jnp.minimum(i, blocks - 1), 0)),
            pl.BlockSpec((parts, BLOCK, width), lambda i: (0, jnp.maximum(i - blocks, 0), 0)),
        ],
        scratch_shapes=[
            pltpu.VMEM((panel, 2 * width), jnp.bfloat16),
            pltpu.VMEM((panel, 2 * width), jnp.bfloat16),
            pltpu.VMEM((panel, 2 * width), jnp.bfloat16),
            pltpu.VMEM((BLOCK, 2 * width), jnp.float32),
        ],
        compiler_params=pltpu.CompilerParams(
            dimension_semantics=("arbitrary",), vmem_limit_bytes=58 << 20
        ),
    )(lin, top, fac, rest)


def tree_body(devices, linv_t, rhs_top, factor_t, rhs_rest):
    lin, fac = gather(devices, linv_t, factor_t)
    return solve(lin, rhs_top, fac, rhs_rest)


def solution(mesh):
    devices = mesh.shape["ang"]
    if mesh.shape["row"] == 1 and devices % 8 == 0:
        body = functools.partial(tree_body, devices)
    else:
        body = general_body
    return jax.shard_map(
        body,
        mesh=mesh,
        in_specs=(
            P(None, "ang", "row"),
            P(None, "row", "ang"),
            P(None, "ang", "row"),
            P(None, "row", "ang"),
        ),
        out_specs=(P(None, "row", "ang"), P(None, "row", "ang")),
        check_vma=False,
    )
```

profile of v0, /device:TPU:0, one launch (start us, length us, event | category | flops | bytes accessed | tf_op | source)
XLA Modules:
  0.0 138.4 jit_solution(1503058296108868781)
XLA Ops:
  0.6 85.6 %shard_map.59 = (bf16[2,2048,2048]{2,1,0:T(8,128)(2,1)}, bf16[2,2048,1024]{2,1,0:T(8,128)(2,1)}) custom-call(bf16[2,64,2048]{2,1,0:T(8,128)(2,1)} %lin_ref.1, bf16[2,64,1024]{2,1,0:T(8,128)(2,1)} %fac_ref.1), custom_call_target="tpu_custom_call" | custom-call | tf_op jit(solution)/shard_map/pallas_call | solution.py:200
  86.3 52.1 %shard_map.60 = (f32[2,2048,512]{2,1,0:T(8,128)}, f32[2,1024,512]{2,1,0:T(8,128)}) custom-call(bf16[2,2048,2048]{2,1,0:T(8,128)(2,1)} %get-tuple-element.4.lin_ref, f32[2,2048,512]{2,1,0:T(8,128)} %top_ref.1, bf16[2,2048,1024]{2,1,0:T(8,128)(2,1)} %get-tuple-element.5.fac_ref, f32[2,1024,512]{2,1,0:T(8,128)} %rest_ref.1), custom_call_target="tpu_custom_call" | custom-call | tf_op jit(solution)/shard_map/pallas_call | solution.py:270
where the time goes:
time: 139 us; the launch traced here: 138 us
  Pallas kernels  138 us (99%)
    pallas_call x1, Pallas kernels, gather(): pl.pallas_call(functools.partial(gather_kernel, devices), out_shape=(jax....  85.6 us
    pallas_call x1, Pallas kernels, solve(): pl.pallas_call(functools.partial(solve_kernel, blocks), grid=(blocks + ta...  52.1 us

commit v1 on v0

v1 whole, which is shorter than its diff:
```python
import functools

import jax
import jax.numpy as jnp
from jax import lax
from jax.experimental import pallas as pl
from jax.experimental.pallas import tpu as pltpu
from jax.sharding import PartitionSpec as P

LAG = 2
KINDS = ((0, 0, "zyx"), (0, 1, "zxy"), (1, 0, "yzx"), (1, 1, "xzy"))
DIMS0 = (((0,), (0,)), ((), ()))


def tdot(first, second):
    return lax.dot_general(first, second, DIMS0, preferred_element_type=jnp.float32)


def split_two(value):
    high = value.astype(jnp.bfloat16)
    low = (value - high.astype(jnp.float32)).astype(jnp.bfloat16)
    return high, low


def general_body(linv_t, rhs_top, factor_t, rhs_rest):
    top_all = lax.all_gather(rhs_top, "row", axis=1, tiled=True)
    high, low = split_two(top_all)
    inverse = lax.all_gather(linv_t, "ang", axis=1, tiled=True)

    def single(first, second):
        return tdot(inverse[first], high[second]) + tdot(inverse[first], low[second])

    solved = jnp.stack([single(0, 0) - single(1, 1), single(0, 1) + single(1, 0)])
    half = lax.all_gather(solved.astype(jnp.bfloat16), "row", axis=1, tiled=True)
    factor = lax.all_gather(factor_t, "ang", axis=1, tiled=True)
    update = jnp.stack(
        [
            tdot(factor[0], half[0]) - tdot(factor[1], half[1]),
            tdot(factor[0], half[1]) + tdot(factor[1], half[0]),
        ]
    )
    return (solved, rhs_rest - update)


def fused_kernel(
    devices, lag, lin_ref, top_ref, fac_ref, rest_ref, solved_ref, updated_ref,
    glin, gfac, high, low, acc, upd, recv, send, local,
):
    levels = devices // 8
    chips = devices // 2
    rows = lin_ref.shape[1]
    panel = lin_ref.shape[2]
    width = top_ref.shape[2]
    block = 4 * rows
    blocks = panel // block
    tail = fac_ref.shape[2] // block

    me = lax.axis_index("ang")
    core = lax.rem(me, 2)
    x = lax.rem(me // 2, 2)
    y = lax.rem(me // 4, 2)
    z = me // 8
    has_up, has_down = z < levels - 1, z > 0
    targets = (
        me + 2 - 4 * x,
        me + 4 - 8 * y,
        jnp.where(has_up, me + 8, me),
        jnp.where(has_down, me - 8, me),
        me + 1 - 2 * core,
    )
    mine = pl.ds(pl.multiple_of(me * rows, rows), rows)

    loads = (
        pltpu.make_async_copy(top_ref.at[0], acc.at[:, pl.ds(0, width)], local.at[0]),
        pltpu.make_async_copy(top_ref.at[1], acc.at[:, pl.ds(width, width)], local.at[1]),
        pltpu.make_async_copy(lin_ref, glin.at[:, mine, :], local.at[2]),
        pltpu.make_async_copy(fac_ref, gfac.at[:, mine, :], local.at[3]),
        pltpu.make_async_copy(rest_ref.at[0], upd.at[:, pl.ds(0, width)], local.at[4]),
        pltpu.make_async_copy(rest_ref.at[1], upd.at[:, pl.ds(width, width)], local.at[5]),
    )

    barrier = pltpu.get_barrier_semaphore()

    def greet(target):
        pl.semaphore_signal(
            barrier, inc=1, device_id={"ang": target}, device_id_type=pl.DeviceIdType.MESH
        )

    for index in (0, 1, 4):
        greet(targets[index])
    pl.when(has_up)(lambda: greet(targets[2]))
    pl.when(has_down)(lambda: greet(targets[3]))
    pl.semaphore_wait(barrier, 3 + has_up.astype(jnp.int32) + has_down.astype(jnp.int32))

    def block_at(index):
        return pl.ds(pl.multiple_of(index * block, block), block)

    def place(kind, origin, cls):
        which, part, _ = KINDS[kind]
        at_rows = pl.ds(pl.multiple_of(origin * rows, rows), rows)
        if which == 0:
            return glin.at[part, at_rows, pl.ds(cls * block, panel - cls * block)]
        return gfac.at[part, at_rows, :]

    def source(kind, cls):
        which, part, _ = KINDS[kind]
        if which == 0:
            return lin_ref.at[part, :, pl.ds(cls * block, panel - cls * block)]
        return fac_ref.at[part]

    def by_class(kind, origin, action):
        if KINDS[kind][0] == 0:
            for cls in range(blocks):
                pl.when(origin // 4 == cls)(functools.partial(action, cls))
        else:
            action(0)

    def remote(kind, origin, cls, direction, own):
        return pltpu.make_async_remote_copy(
            src_ref=source(kind, cls) if own else place(kind, origin, cls),
            dst_ref=place(kind, origin, cls),
            send_sem=send.at[direction, kind, origin // 2],
            recv_sem=recv.at[kind, origin],
            device_id={"ang": targets[direction]},
            device_id_type=pl.DeviceIdType.MESH,
        )

    def onward(kind, zo, yo, xo):
        same = {"x": x == xo, "y": y == yo, "z": z == zo}
        order = KINDS[kind][2]
        free = {}
        for position, axis in enumerate(order):
            ok = True
            for later in order[position + 1 :]:
                ok = same[later] if ok is True else jnp.logical_and(ok, same[later])
            free[axis] = ok

        def both(first, second):
            return second if first is True else jnp.logical_and(first, second)

        return (
            both(free["x"], same["x"]),
            both(free["y"], same["y"]),
            both(free["z"], jnp.logical_and(z >= zo, has_up)),
            both(free["z"], jnp.logical_and(z <= zo, has_down)),
            True,
        )

    def forward(kind, origin, goes, cls, own, act):
        for direction in range(5):
            copy = remote(kind, origin, cls, direction, own)
            run = copy.start if act == "start" else copy.wait_send
            if goes[direction] is True:
                run()
            else:
                pl.when(goes[direction])(run)

    def send_own(kind):
        goes = onward(kind, z, y, x)
        by_class(kind, me, lambda cls: forward(kind, me, goes, cls, True, "start"))

    def arrive_other(kind, origin):
        by_class(kind, origin, lambda cls: remote(kind, origin, cls, 4, False).wait_recv())

    send_own(0)
    send_own(1)
    for copy in loads:
        copy.start()
    loads[0].wait()
    loads[1].wait()

    @pl.loop(0, blocks)
    def _(index):
        at_rows = block_at(index)
        for part in range(2):
            cols = slice(part * width, (part + 1) * width)
            first, second = split_two(acc[at_rows, cols])
            high[at_rows, cols] = first
            low[at_rows, cols] = second
        acc[at_rows, :] = jnp.zeros((block, 2 * width), jnp.float32)

    for copy in loads[2:]:
        copy.wait()

    def solve_piece(group, index):
        at_rows, at_cols, to = block_at(group), block_at(index), block_at(index)
        lreal, limag = glin[0, at_rows, at_cols], glin[1, at_rows, at_cols]
        first, second = high[at_rows, :], low[at_rows, :]
        real = tdot(lreal, first) + tdot(lreal, second)
        imag = tdot(limag, first) + tdot(limag, second)
        acc[to, :width] += real[:, :width] - imag[:, width:]
        acc[to, width:] += real[:, width:] + imag[:, :width]

    def update_piece(group, index):
        at_rows, at_cols, to = block_at(group), block_at(index), block_at(index)
        right = high[at_rows, :]
        real = tdot(gfac[0, at_rows, at_cols], right)
        imag = tdot(gfac[1, at_rows, at_cols], right)
        upd[to, :width] += imag[:, width:] - real[:, :width]
        upd[to, width:] -= real[:, width:] + imag[:, :width]

    stores = (
        pltpu.make_async_copy(acc.at[:, pl.ds(0, width)], solved_ref.at[0], local.at[0]),
        pltpu.make_async_copy(acc.at[:, pl.ds(width, width)], solved_ref.at[1], local.at[1]),
        pltpu.make_async_copy(upd.at[:, pl.ds(0, width)], updated_ref.at[0], local.at[2]),
        pltpu.make_async_copy(upd.at[:, pl.ds(width, width)], updated_ref.at[1], local.at[3]),
    )
    solved_at = levels + 3

    def apart(group):
        return jnp.abs(z - group // 2) + jnp.abs(y - lax.rem(group, 2))

    def first_round(group):
        return jnp.maximum(apart(group) + 2 + lag, solved_at)

    def visit(step, carry):
        turn = step // chips
        chip = lax.rem(step, chips)
        zo, yo, xo = chip // 4, lax.rem(chip // 2, 2), lax.rem(chip, 2)
        distance = jnp.abs(z - zo) + jnp.abs(y - yo) + jnp.abs(x - xo)
        origin = chip * 2 + core
        other = chip * 2 + 1 - core

        @pl.when(chip == 0)
        def _():
            @pl.when(turn == lag)
            def _():
                send_own(2)
                send_own(3)

            @pl.when(turn == solved_at)
            def _():
                @pl.loop(0, blocks)
                def _(index):
                    high[block_at(index), :] = acc[block_at(index), :].astype(jnp.bfloat16)

                stores[0].start()
                stores[1].start()

            def arrivals(index, carry):
                group = index // 4

                @pl.when(apart(group) + 2 == turn)
                def _():
                    @pl.when(lax.rem(index, 2) == 1 - core)
                    def _():
                        arrive_other(0, index)
                        arrive_other(1, index)

                @pl.when(first_round(group) == turn)
                def _():
                    @pl.when(lax.rem(index, 2) == 1 - core)
                    def _():
                        arrive_other(2, index)
                        arrive_other(3, index)

                return carry

            lax.fori_loop(0, devices, arrivals, 0)

        for kinds, hops in (((0, 1), turn), ((2, 3), turn - lag)):

            @pl.when(jnp.logical_and(distance == hops, hops > 0))
            def _(kinds=kinds):
                for kind in kinds:
                    goes = onward(kind, zo, yo, xo)

                    def arrive(cls, kind=kind, goes=goes):
                        remote(kind, origin, cls, 4, False).wait_recv()
                        forward(kind, origin, goes, cls, False, "start")

                    by_class(kind, origin, arrive)

        @pl.when(lax.rem(chip, 2) == 0)
        def _():
            index = chip // 2

            @pl.loop(0, blocks)
            def _(group):
                @pl.when(jnp.logical_and(apart(group) + 2 == turn, index >= group))
                def _():
                    solve_piece(group, index)

        every = chips // tail

        @pl.when(lax.rem(chip, every) == 0)
        def _():
            index = chip // every

            @pl.loop(0, blocks)
            def _(group):
                @pl.when(first_round(group) == turn)
                def _():
                    update_piece(group, index)

        return carry

    lax.fori_loop(chips, chips * (levels + 3 + lag), visit, 0)

    stores[2].start()
    stores[3].start()

    def finish(chip, carry):
        zo, yo, xo = chip // 4, lax.rem(chip // 2, 2), lax.rem(chip, 2)
        origin = chip * 2 + core
        for kind in range(4):
            goes = onward(kind, zo, yo, xo)
            by_class(
                kind,
                origin,
                lambda cls, kind=kind, goes=goes: forward(kind, origin, goes, cls, False, "wait"),
            )
        return carry

    lax.fori_loop(0, chips, finish, 0)
    for copy in stores:
        copy.wait()


def fused_body(devices, linv_t, rhs_top, factor_t, rhs_rest):
    parts, rows, panel = linv_t.shape
    trail, width = rhs_rest.shape[1:]
    return pl.pallas_call(
        functools.partial(fused_kernel, devices, LAG),
        out_shape=(
            jax.ShapeDtypeStruct(rhs_top.shape, jnp.float32),
            jax.ShapeDtypeStruct(rhs_rest.shape, jnp.float32),
        ),
        in_specs=[pl.BlockSpec(memory_space=pl.ANY)] * 4,
        out_specs=[pl.BlockSpec(memory_space=pl.ANY)] * 2,
        scratch_shapes=[
            pltpu.VMEM((parts, panel, panel), linv_t.dtype),
            pltpu.VMEM((parts, panel, trail), factor_t.dtype),
            pltpu.VMEM((panel, 2 * width), jnp.bfloat16),
            pltpu.VMEM((panel, 2 * width), jnp.bfloat16),
            pltpu.VMEM((panel, 2 * width), jnp.float32),
            pltpu.VMEM((trail, 2 * width), jnp.float32),
            pltpu.SemaphoreType.DMA((4, devices)),
            pltpu.SemaphoreType.DMA((5, 4, devices // 2)),
            pltpu.SemaphoreType.DMA((6,)),
        ],
        compiler_params=pltpu.CompilerParams(
            collective_id=0, has_side_effects=True, vmem_limit_bytes=60 << 20
        ),
    )(linv_t, rhs_top, factor_t, rhs_rest)


def solution(mesh):
    devices = mesh.shape["ang"]
    if mesh.shape["row"] == 1 and devices % 8 == 0:
        body = functools.partial(fused_body, devices)
    else:
        body = general_body
    return jax.shard_map(
        body,
        mesh=mesh,
        in_specs=(
            P(None, "ang", "row"),
            P(None, "row", "ang"),
            P(None, "ang", "row"),
            P(None, "row", "ang"),
        ),
        out_specs=(P(None, "row", "ang"), P(None, "row", "ang")),
        check_vma=False,
    )
```

time: 139 us -> 133 us (0.957)
  the two profiles are of different devices: /device:TPU:0 before, /device:TPU:30 now
where the time goes in v1:
time: 133 us
  Pallas kernels  122 us (92%)
  local copies, waits for them, and re-layouts  9.96 us (7%)
    pallas_call x1, Pallas kernels, fused_body(): pl.pallas_call(functools.partial(fused_kernel, devices, LAG), out_shape=(...  122 us
    unnamed x4, local copies, waits for them, and re-layouts  9.96 us

profile of v1, /device:TPU:30, one launch (start us, length us, event | category | flops | bytes accessed | tf_op | source)
XLA Modules:
  0.0 132.6 jit_solution(12108163262889273851)
XLA Ops:
  0.6 122.0 %shard_map.59 = (f32[2,2048,512]{2,1,0:T(8,128)}, f32[2,1024,512]{2,1,0:T(8,128)}) custom-call(bf16[2,64,2048]{2,1,0:T(8,128)(2,1)} %lin_ref.1, f32[2,2048,512]{2,1,0:T(8,128)} %top_ref.1, bf16[2,64,1024]{2,1,0:T(8,128)(2,1)} %fac_ref.1, f32[2,1024,512]{2,1,0:T(8,128)} %rest_ref.1), custom_call_target="tpu_custom_call" | custom-call | tf_op jit(solution)/shard_map/pallas_call | solution.py:323
  122.6 0.0 copy-start
  122.7 7.9 %copy.8 = f32[2,2048,512]{2,1,0:T(8,128)} copy(f32[2,2048,512]{2,1,0:T(8,128)} %get-tuple-element.4) | data formatting | bytes 16777216
  130.6 0.0 copy-done
  130.6 2.0 %copy.9 = f32[2,1024,512]{2,1,0:T(8,128)} copy(f32[2,1024,512]{2,1,0:T(8,128)S(1)} %copy-done) | data formatting | bytes 8388608
Async XLA Ops:
  122.6 8.0 %copy-start = (f32[2,1024,512]{2,1,0:T(8,128)S(1)}, f32[2,1024,512]{2,1,0:T(8,128)}, u32[]{:S(2)}) copy-start(f32[2,1024,512]{2,1,0:T(8,128)} %get-tuple-element.5) | copy-start | bytes 12582916

commit v2 on v1

--- a/solution.py
+++ b/solution.py
@@ -7,7 +7,7 @@
 from jax.experimental.pallas import tpu as pltpu
 from jax.sharding import PartitionSpec as P
 
-LAG = 2
+LAG = 1
 KINDS = ((0, 0, "zyx"), (0, 1, "zxy"), (1, 0, "yzx"), (1, 1, "xzy"))
 DIMS0 = (((0,), (0,)), ((), ()))
 
@@ -44,7 +44,7 @@
 
 def fused_kernel(
     devices, lag, lin_ref, top_ref, fac_ref, rest_ref, solved_ref, updated_ref,
-    glin, gfac, high, low, acc, upd, recv, send, local,
+    glin, gfac, terms, acc, upd, recv, send, local,
 ):
     levels = devices // 8
     chips = devices // 2
@@ -71,12 +71,10 @@
     mine = pl.ds(pl.multiple_of(me * rows, rows), rows)
 
     loads = (
-        pltpu.make_async_copy(top_ref.at[0], acc.at[:, pl.ds(0, width)], local.at[0]),
-        pltpu.make_async_copy(top_ref.at[1], acc.at[:, pl.ds(width, width)], local.at[1]),
-        pltpu.make_async_copy(lin_ref, glin.at[:, mine, :], local.at[2]),
-        pltpu.make_async_copy(fac_ref, gfac.at[:, mine, :], local.at[3]),
-        pltpu.make_async_copy(rest_ref.at[0], upd.at[:, pl.ds(0, width)], local.at[4]),
-        pltpu.make_async_copy(rest_ref.at[1], upd.at[:, pl.ds(width, width)], local.at[5]),
+        pltpu.make_async_copy(top_ref, acc, local.at[0]),
+        pltpu.make_async_copy(lin_ref, glin.at[:, mine, :], local.at[1]),
+        pltpu.make_async_copy(fac_ref, gfac.at[:, mine, :], local.at[2]),
+        pltpu.make_async_copy(rest_ref, upd, local.at[3]),
     )
 
     barrier = pltpu.get_barrier_semaphore()
@@ -167,44 +165,66 @@
     for copy in loads:
         copy.start()
     loads[0].wait()
-    loads[1].wait()
 
     @pl.loop(0, blocks)
     def _(index):
         at_rows = block_at(index)
         for part in range(2):
-            cols = slice(part * width, (part + 1) * width)
-            first, second = split_two(acc[at_rows, cols])
-            high[at_rows, cols] = first
-            low[at_rows, cols] = second
-        acc[at_rows, :] = jnp.zeros((block, 2 * width), jnp.float32)
-
-    for copy in loads[2:]:
+            first, second = split_two(acc[part, at_rows, :])
+            terms[pl.ds(pl.multiple_of((4 * index + 2 * part) * block, block), block), :] = first
+            terms[pl.ds(pl.multiple_of((4 * index + 2 * part + 1) * block, block), block), :] = second
+            acc[part, at_rows, :] = jnp.zeros((block, width), jnp.float32)
+
+    for copy in loads[1:]:
         copy.wait()
 
     def solve_piece(group, index):
-        at_rows, at_cols, to = block_at(group), block_at(index), block_at(index)
-        lreal, limag = glin[0, at_rows, at_cols], glin[1, at_rows, at_cols]
-        first, second = high[at_rows, :], low[at_rows, :]
-        real = tdot(lreal, first) + tdot(lreal, second)
-        imag = tdot(limag, first) + tdot(limag, second)
-        acc[to, :width] += real[:, :width] - imag[:, width:]
-        acc[to, width:] += real[:, width:] + imag[:, :width]
+        at_rows, to = block_at(group), block_at(index)
+        lreal, limag = glin[0, at_rows, to].T, glin[1, at_rows, to].T
+        right = terms[pl.ds(pl.multiple_of(4 * group * block, block), 4 * block), :]
+        real = jnp.concatenate([lreal, lreal, -limag, -limag], axis=1)
+        imag = jnp.concatenate([limag, limag, lreal, lreal], axis=1)
+        both = jnp.dot(
+            jnp.concatenate([real, imag]), right, preferred_element_type=jnp.float32
+        )
+        acc[0, to, :] += both[:block]
+        acc[1, to, :] += both[block:]
 
     def update_piece(group, index):
-        at_rows, at_cols, to = block_at(group), block_at(index), block_at(index)
-        right = high[at_rows, :]
-        real = tdot(gfac[0, at_rows, at_cols], right)
-        imag = tdot(gfac[1, at_rows, at_cols], right)
-        upd[to, :width] += imag[:, width:] - real[:, :width]
-        upd[to, width:] -= real[:, width:] + imag[:, :width]
+        at_rows, to = block_at(group), block_at(index)
+        freal, fimag = gfac[0, at_rows, to].T, gfac[1, at_rows, to].T
+        right = terms[pl.ds(pl.multiple_of(2 * group * block, block), 2 * block), :]
+        real = jnp.concatenate([freal, -fimag], axis=1)
+        imag = jnp.concatenate([fimag, freal], axis=1)
+        both = jnp.dot(
+            jnp.concatenate([real, imag]), right, preferred_element_type=jnp.float32
+        )
+        upd[0, to, :] -= both[:block]
+        upd[1, to, :] -= both[block:]
+
+    def update_block(index):
+        to = block_at(index)
+        freal, fimag = gfac[0, :, to].T, gfac[1, :, to].T
+        lines = []
+        for first, second in ((freal, -fimag), (fimag, freal)):
+            pieces = []
+            for group in range(blocks):
+                cols = slice(group * block, (group + 1) * block)
+                pieces += [first[:, cols], second[:, cols]]
+            lines.append(jnp.concatenate(pieces, axis=1))
+        both = jnp.dot(
+            jnp.concatenate(lines),
+            terms[pl.ds(0, 2 * panel), :],
+            preferred_element_type=jnp.float32,
+        )
+        upd[0, to, :] -= both[:block]
+        upd[1, to, :] -= both[block:]
 
     stores = (
-        pltpu.make_async_copy(acc.at[:, pl.ds(0, width)], solved_ref.at[0], local.at[0]),
-        pltpu.make_async_copy(acc.at[:, pl.ds(width, width)], solved_ref.at[1], local.at[1]),
-        pltpu.make_async_copy(upd.at[:, pl.ds(0, width)], updated_ref.at[0], local.at[2]),
-        pltpu.make_async_copy(upd.at[:, pl.ds(width, width)], updated_ref.at[1], local.at[3]),
+        pltpu.make_async_copy(acc, solved_ref, local.at[0]),
+        pltpu.make_async_copy(upd, updated_ref, local.at[1]),
     )
+    last_round = levels + 2 + lag
     solved_at = levels + 3
 
     def apart(group):
@@ -213,92 +233,124 @@
     def first_round(group):
         return jnp.maximum(apart(group) + 2 + lag, solved_at)
 
-    def visit(step, carry):
-        turn = step // chips
-        chip = lax.rem(step, chips)
+    def solve_count(group, turn):
+        return jnp.where(apart(group) + 2 == turn, blocks - group, 0)
+
+    def update_count(group, turn):
+        return jnp.where(jnp.logical_and(turn == last_round, group < tail), 1, 0)
+
+    def run_pieces(turn, first, last):
+        def find(number, count):
+            def scan(group, carry):
+                rest, found = carry
+                size = count(group, turn)
+                found = jnp.where(jnp.logical_and(found < 0, rest < size), group, found)
+                return jnp.where(found < 0, rest - size, rest), found
+
+            return lax.fori_loop(0, blocks, scan, (number, jnp.int32(-1)))
+
+        @pl.when(turn < solved_at)
+        def _():
+            @pl.loop(first, last)
+            def _(number):
+                rest, group = find(number, solve_count)
+                solve_piece(group, group + rest)
+
+        @pl.when(turn >= solved_at)
+        def _():
+            @pl.loop(first, last)
+            def _(number):
+                rest, group = find(number, update_count)
+                update_block(group)
+
+    def distance_to(chip):
         zo, yo, xo = chip // 4, lax.rem(chip // 2, 2), lax.rem(chip, 2)
-        distance = jnp.abs(z - zo) + jnp.abs(y - yo) + jnp.abs(x - xo)
-        origin = chip * 2 + core
-        other = chip * 2 + 1 - core
-
-        @pl.when(chip == 0)
+        return jnp.abs(z - zo) + jnp.abs(y - yo) + jnp.abs(x - xo)
+
+    def in_round(chip, turn):
+        distance = distance_to(chip)
+        first = distance == turn
+        second = jnp.logical_and(distance == turn - lag, turn > lag)
+        return first, second
+
+    def one_round(turn, carry):
+        @pl.when(turn == lag)
         def _():
-            @pl.when(turn == lag)
+            send_own(2)
+            send_own(3)
+
+        @pl.when(turn == solved_at)
+        def _():
+            @pl.loop(0, blocks)
+            def _(index):
+                for part in range(2):
+                    to = pl.ds(pl.multiple_of((2 * index + part) * block, block), block)
+                    terms[to, :] = acc[part, block_at(index), :].astype(jnp.bfloat16)
+
+            stores[0].start()
+
+        def arrivals(chip, carry):
+            other = chip * 2 + 1 - core
+            group = chip // 2
+
+            @pl.when(apart(group) + 2 == turn)
             def _():
-                send_own(2)
-                send_own(3)
-
-            @pl.when(turn == solved_at)
+                arrive_other(0, other)
+                arrive_other(1, other)
+
+            @pl.when(first_round(group) == turn)
             def _():
-                @pl.loop(0, blocks)
-                def _(index):
-                    high[block_at(index), :] = acc[block_at(index), :].astype(jnp.bfloat16)
-
-                stores[0].start()
-                stores[1].start()
-
-            def arrivals(index, carry):
-                group = index // 4
-
-                @pl.when(apart(group) + 2 == turn)
-                def _():
-                    @pl.when(lax.rem(index, 2) == 1 - core)
-                    def _():
-                        arrive_other(0, index)
-                        arrive_other(1, index)
-
-                @pl.when(first_round(group) == turn)
-                def _():
-                    @pl.when(lax.rem(index, 2) == 1 - core)
-                    def _():
-                        arrive_other(2, index)
-                        arrive_other(3, index)
-
-                return carry
-
-            lax.fori_loop(0, devices, arrivals, 0)
-
-        for kinds, hops in (((0, 1), turn), ((2, 3), turn - lag)):
-
-            @pl.when(jnp.logical_and(distance == hops, hops > 0))
-            def _(kinds=kinds):
-                for kind in kinds:
-                    goes = onward(kind, zo, yo, xo)
-
-                    def arrive(cls, kind=kind, goes=goes):
-                        remote(kind, origin, cls, 4, False).wait_recv()
-                        forward(kind, origin, goes, cls, False, "start")
-
-                    by_class(kind, origin, arrive)
-
-        @pl.when(lax.rem(chip, 2) == 0)
-        def _():
-            index = chip // 2
-
-            @pl.loop(0, blocks)
-            def _(group):
-                @pl.when(jnp.logical_and(apart(group) + 2 == turn, index >= group))
-                def _():
-                    solve_piece(group, index)
-
-        every = chips // tail
-
-        @pl.when(lax.rem(chip, every) == 0)
-        def _():
-            index = chip // every
-
-            @pl.loop(0, blocks)
-            def _(group):
-                @pl.when(first_round(group) == turn)
-                def _():
-                    update_piece(group, index)
-
+                arrive_other(2, other)
+                arrive_other(3, other)
+
+            return carry
+
+        lax.fori_loop(0, chips, arrivals, 0)
+
+        def add_pieces(group, total):
+            return total + jnp.where(
+                turn < solved_at, solve_count(group, turn), update_count(group, turn)
+            )
+
+        def add_events(chip, total):
+            first, second = in_round(chip, turn)
+            return total + jnp.where(jnp.logical_or(first, second), 1, 0)
+
+        pieces = lax.fori_loop(0, blocks, add_pieces, jnp.int32(0))
+        slots = lax.fori_loop(0, chips, add_events, jnp.int32(1))
+
+        def visit(chip, slot):
+            zo, yo, xo = chip // 4, lax.rem(chip // 2, 2), lax.rem(chip, 2)
+            origin = chip * 2 + core
+            first, second = in_round(chip, turn)
+            either = jnp.logical_or(first, second)
+
+            for kinds, now in (((0, 1), first), ((2, 3), second)):
+
+                @pl.when(now)
+                def _(kinds=kinds):
+                    for kind in kinds:
+                        goes = onward(kind, zo, yo, xo)
+
+                        def arrive(cls, kind=kind, goes=goes):
+                            remote(kind, origin, cls, 4, False).wait_recv()
+                            forward(kind, origin, goes, cls, False, "start")
+
+                        by_class(kind, origin, arrive)
+
+            @pl.when(either)
+            def _():
+                run_pieces(turn, slot * pieces // slots, (slot + 1) * pieces // slots)
+
+            return slot + jnp.where(either, 1, 0)
+
+        lax.fori_loop(0, chips, visit, jnp.int32(0))
+        run_pieces(turn, (slots - 1) * pieces // slots, pieces)
         return carry
 
-    lax.fori_loop(chips, chips * (levels + 3 + lag), visit, 0)
-
-    stores[2].start()
-    stores[3].start()
+    lax.fori_loop(1, levels + 3 + lag, one_round, 0)
+
+    stores[1].start()
 
     def finish(chip, carry):
         zo, yo, xo = chip // 4, lax.rem(chip // 2, 2), lax.rem(chip, 2)
@@ -331,13 +383,12 @@
         scratch_shapes=[
             pltpu.VMEM((parts, panel, panel), linv_t.dtype),
             pltpu.VMEM((parts, panel, trail), factor_t.dtype),
-            pltpu.VMEM((panel, 2 * width), jnp.bfloat16),
-            pltpu.VMEM((panel, 2 * width), jnp.bfloat16),
-            pltpu.VMEM((panel, 2 * width), jnp.float32),
-            pltpu.VMEM((trail, 2 * width), jnp.float32),
+            pltpu.VMEM((4 * panel, width), jnp.bfloat16),
+            pltpu.VMEM(rhs_top.shape, jnp.float32),
+            pltpu.VMEM(rhs_rest.shape, jnp.float32),
             pltpu.SemaphoreType.DMA((4, devices)),
             pltpu.SemaphoreType.DMA((5, 4, devices // 2)),
-            pltpu.SemaphoreType.DMA((6,)),
+            pltpu.SemaphoreType.DMA((4,)),
         ],
         compiler_params=pltpu.CompilerParams(
             collective_id=0, has_side_effects=True, vmem_limit_bytes=60 << 20

time: 133 us -> 118 us (0.89)
  Pallas kernels: 122 us -> 107 us
    pallas_call x1, Pallas kernels: 122 us -> 107 us  [fused_body(): pl.pallas_call(functools.partial(fused_kernel, devices, LAG), out_shape=(...]
where the time goes in v2:
time: 118 us
  Pallas kernels  107 us (91%)
  local copies, waits for them, and re-layouts  9.96 us (8%)
    pallas_call x1, Pallas kernels, fused_body(): pl.pallas_call(functools.partial(fused_kernel, devices, LAG), out_shape=(...  107 us
    unnamed x4, local copies, waits for them, and re-layouts  9.96 us

profile of v2, /device:TPU:30, one launch (start us, length us, event | category | flops | bytes accessed | tf_op | source)
XLA Modules:
  0.0 117.5 jit_solution(17084986994564230112)
XLA Ops:
  0.6 106.9 %shard_map.59 = (f32[2,2048,512]{2,1,0:T(8,128)}, f32[2,1024,512]{2,1,0:T(8,128)}) custom-call(bf16[2,64,2048]{2,1,0:T(8,128)(2,1)} %lin_ref.1, f32[2,2048,512]{2,1,0:T(8,128)} %top_ref.1, bf16[2,64,1024]{2,1,0:T(8,128)(2,1)} %fac_ref.1, f32[2,1024,512]{2,1,0:T(8,128)} %rest_ref.1), custom_call_target="tpu_custom_call" | custom-call | tf_op jit(solution)/shard_map/pallas_call | solution.py:375
  107.5 0.0 copy-start
  107.6 7.9 %copy.8 = f32[2,2048,512]{2,1,0:T(8,128)} copy(f32[2,2048,512]{2,1,0:T(8,128)} %get-tuple-element.4) | data formatting | bytes 16777216
  115.5 0.0 copy-done
  115.5 2.0 %copy.9 = f32[2,1024,512]{2,1,0:T(8,128)} copy(f32[2,1024,512]{2,1,0:T(8,128)S(1)} %copy-done) | data formatting | bytes 8388608
Async XLA Ops:
  107.5 8.0 %copy-start = (f32[2,1024,512]{2,1,0:T(8,128)S(1)}, f32[2,1024,512]{2,1,0:T(8,128)}, u32[]{:S(2)}) copy-start(f32[2,1024,512]{2,1,0:T(8,128)} %get-tuple-element.5) | copy-start | bytes 12582916
